TPU v7x, 32 devices: a whole 2x2x4 slice. The times are simulated.
32 devices in a mesh: rep: 8 (over y, x, core), shard: 4 (over z).
Axes of the slice: x: 2, y: 2, z: 4, core: 2. Of those that a mesh axis runs over, the one named last changes fastest.
Arguments:
- tokens: bfloat16 [16384, 1536], P(('rep', 'shard')), may hold values from -6 to 6
- cotangent: bfloat16 [16384, 1536], P(('rep', 'shard')), may hold values from -6 to 6
- norm_first: bfloat16 [1536], P('shard'), may hold values from 0.5 to 1.5
- branch_weight: bfloat16 [1536, 2048], P(None, 'shard'), may hold values from -0.15625 to 0.15625
- gelu_weight: bfloat16 [1536, 2048], P(None, 'shard'), may hold values from -0.15625 to 0.15625
- conv_weight: bfloat16 [4, 2048], P(None, 'shard'), may hold values from -2.5 to 2.5
- conv_bias: bfloat16 [2048], P('shard'), may hold values from -2.5 to 2.5
- gate_weight: bfloat16 [16, 128, 256], P('shard'), may hold values from -0.5 to 0.5
- gate_bias: bfloat16 [16, 256], P('shard'), may hold values from -2.5 to 2.5
- decay_param: bfloat16 [2048], P('shard'), may hold values from 2.1875 to 6.875
- merge_weight: bfloat16 [2048, 1536], P('shard'), may hold values from -0.375 to 0.375
- norm_second: bfloat16 [1536], P('shard'), may hold values from 0.5 to 1.5
- feed_gate: bfloat16 [1536, 4608], P(None, 'shard'), may hold values from -0.15625 to 0.15625
- feed_up: bfloat16 [1536, 4608], P(None, 'shard'), may hold values from -0.15625 to 0.15625
- feed_down: bfloat16 [4608, 1536], P('shard'), may hold values from -0.1875 to 0.1875
- down_branch: bfloat16 [1536, 128], P(None, 'shard'), may hold values from -0.15625 to 0.15625
- up_branch: bfloat16 [128, 2048], P('shard'), may hold values from -0.75 to 0.75
- down_gelu: bfloat16 [1536, 128], P(None, 'shard'), may hold values from -0.15625 to 0.15625
- up_gelu: bfloat16 [128, 2048], P('shard'), may hold values from -0.75 to 0.75
- down_gates: bfloat16 [2048, 128], P(None, 'shard'), may hold values from -0.125 to 0.125
- up_gates: bfloat16 [128, 4096], P('shard'), may hold values from -0.75 to 0.75
- down_merge: bfloat16 [2048, 128], P(None, 'shard'), may hold values from -0.125 to 0.125
- up_merge: bfloat16 [128, 1536], P('shard'), may hold values from -0.75 to 0.75
- down_feed_gate: bfloat16 [1536, 128], P(None, 'shard'), may hold values from -0.15625 to 0.15625
- up_feed_gate: bfloat16 [128, 4608], P('shard'), may hold values from -0.75 to 0.75
- down_feed_up: bfloat16 [1536, 128], P(None, 'shard'), may hold values from -0.15625 to 0.15625
- up_feed_up: bfloat16 [128, 4608], P('shard'), may hold values from -0.75 to 0.75
- down_feed_down: bfloat16 [4608, 128], P(None, 'shard'), may hold values from -0.09375 to 0.09375
- up_feed_down: bfloat16 [128, 1536], P('shard'), may hold values from -0.75 to 0.75
- seq_lengths: int32 [32, 4], P(('rep', 'shard')), may hold values from 1 to 256, 384 in all within a row
- adapter_index: int32 [32, 4], P(('rep', 'shard')), may hold values from 0 to 7
- deal_order: int32 [8, 2048], P('rep'), may hold values from 0 to 2047, as said below
Outputs:
- layer_out: float32 [16384, 1536], P(('rep', 'shard'))
- grad_tokens: float32 [16384, 1536], P(('rep', 'shard'))
- grad_down_branch: float32 [1536, 128], P(None, 'shard')
- grad_up_branch: float32 [128, 2048], P('shard')
- grad_down_gelu: float32 [1536, 128], P(None, 'shard')
- grad_up_gelu: float32 [128, 2048], P('shard')
- grad_down_gates: float32 [2048, 128], P(None, 'shard')
- grad_up_gates: float32 [128, 4096], P('shard')
- grad_down_merge: float32 [2048, 128], P(None, 'shard')
- grad_up_merge: float32 [128, 1536], P('shard')
- grad_down_feed_gate: float32 [1536, 128], P(None, 'shard')
- grad_up_feed_gate: float32 [128, 4608], P('shard')
- grad_down_feed_up: float32 [1536, 128], P(None, 'shard')
- grad_up_feed_up: float32 [128, 4608], P('shard')
- grad_down_feed_down: float32 [4608, 128], P(None, 'shard')
- grad_up_feed_down: float32 [128, 1536], P('shard')
Inputs may be any that keep to these rules, and one draw needn't show every extreme that they name: Each row of deal_order is a permutation of 0 to 2047. Exactly 128 of the arrival rows of one device (rows b * 512 to b * 512 + 511 of its group) fill slots of each block of its group. `seq_lengths`: in every block the lengths sum to 384 and the longest is 256.
All inputs are finite; a program needn't handle non-finite values.
Results may differ from a plain program's by a relative error of at most 0.015.
Values may be sent and summed in bfloat16 or wider, within the bound.
A program may use at most 320 MiB of HBM per device.

v0:
```python
import jax
import jax.numpy as jnp
from jax import lax
from jax.sharding import PartitionSpec as P

H = 16
DH = 128
NA = 8
R = 16
NORM_EPSILON = 1e-06
DECAY_SCALE = 8.0


def matmul(left, right):
    return jnp.dot(left, right, preferred_element_type=jnp.float32)


def matmul_right_t(left, right):
    return lax.dot_general(
        left, right, (((1,), (1,)), ((), ())), preferred_element_type=jnp.float32
    )


def matmul_left_t(left, right):
    return lax.dot_general(
        left, right, (((0,), (0,)), ((), ())), preferred_element_type=jnp.float32
    )


def root_norm(values, gain):
    return (
        values * lax.rsqrt(jnp.mean(values * values, axis=-1, keepdims=True) + NORM_EPSILON) * gain
    )


def layout(lengths_row, index_row, slots_count):
    seq_count = lengths_row.shape[0]
    ends = jnp.cumsum(lengths_row)
    starts = ends - lengths_row
    slots = jnp.arange(slots_count, dtype=jnp.int32)
    segment = jnp.sum((slots[:, None] >= ends[None, :]).astype(jnp.int32), axis=1)
    start_all = jnp.concatenate([starts, ends[-1:]])
    member = segment[:, None] == jnp.arange(seq_count + 1, dtype=jnp.int32)[None, :]
    position = slots - jnp.sum(jnp.where(member, start_all[None, :], 0), axis=1)
    live_rows = segment < seq_count
    chosen = jnp.sum(jnp.where(member[:, :seq_count], index_row[None, :], 0), axis=1)
    adapter_hit = (chosen[:, None] == jnp.arange(NA, dtype=jnp.int32)[None, :]) & live_rows[:, None]
    adapter_mask = jnp.repeat(adapter_hit.astype(jnp.float32), R, axis=1)
    return (position, live_rows.astype(jnp.float32), adapter_mask)


def conv_apply(values, weight, bias, position):
    total = bias[None, :] + weight[0][None, :] * values
    for offset in range(1, weight.shape[0]):
        moved = jnp.concatenate(
            [jnp.zeros((offset, values.shape[1]), values.dtype), values[:-offset]], axis=0
        )
        keeper = (position >= offset).astype(values.dtype)[:, None]
        total = total + weight[offset][None, :] * moved * keeper
    return total


def combine(earlier, later):
    return (earlier[0] * later[0], later[0] * earlier[1] + later[1])


def recurrence(gate_logits, conv_out, gelu_in, decay, position):
    rows_count = conv_out.shape[0]
    shaped = gate_logits.reshape(rows_count, H, 2 * DH)
    input_gate = jax.nn.sigmoid(shaped[:, :, :DH]).reshape(rows_count, H * DH)
    rec_gate = jax.nn.sigmoid(shaped[:, :, DH:]).reshape(rows_count, H * DH)
    log_decay = -DECAY_SCALE * rec_gate * jax.nn.softplus(-decay)[None, :]
    decay_now = jnp.exp(log_decay)
    first = (position == 0)[:, None]
    scale_in = jnp.where(first, 1.0, jnp.sqrt(-jnp.expm1(2.0 * log_decay)))
    carried = jnp.where(first, 0.0, decay_now)
    driven = scale_in * input_gate * conv_out
    unused, state = lax.associative_scan(combine, (carried, driven), axis=0)
    return state * jax.nn.gelu(gelu_in)


def feed_mix(hidden_gate, hidden_up):
    return jax.nn.gelu(hidden_gate) * hidden_up


def local(
    tokens,
    cotangent,
    norm_first,
    branch_weight,
    gelu_weight,
    conv_weight,
    conv_bias,
    gate_weight,
    gate_bias,
    decay_param,
    merge_weight,
    norm_second,
    feed_gate,
    feed_up,
    feed_down,
    down_branch,
    up_branch,
    down_gelu,
    up_gelu,
    down_gates,
    up_gates,
    down_merge,
    up_merge,
    down_feed_gate,
    up_feed_gate,
    down_feed_up,
    up_feed_up,
    down_feed_down,
    up_feed_down,
    seq_lengths,
    adapter_index,
    deal_order,
):
    rows_here = tokens.shape[0]
    shards = lax.axis_size("shard")
    my_index = lax.axis_index("shard")
    deal_row = deal_order[0]
    group_rows = deal_row.shape[0]
    gathered = (
        lax.all_gather(tokens, "shard", axis=0, tiled=True),
        lax.all_gather(cotangent, "shard", axis=0, tiled=True),
    )
    my_picks = lax.dynamic_slice_in_dim(deal_row, my_index * rows_here, rows_here)
    work_in = jnp.take(gathered[0], my_picks, axis=0)
    work_cot = jnp.take(gathered[1], my_picks, axis=0)
    block_parts = (
        lax.all_gather(norm_first, "shard", axis=0, tiled=True),
        lax.all_gather(branch_weight, "shard", axis=1, tiled=True),
        lax.all_gather(gelu_weight, "shard", axis=1, tiled=True),
        lax.all_gather(conv_weight, "shard", axis=1, tiled=True),
        lax.all_gather(conv_bias, "shard", axis=0, tiled=True),
        lax.all_gather(gate_weight, "shard", axis=0, tiled=True),
        lax.all_gather(gate_bias, "shard", axis=0, tiled=True),
        lax.all_gather(decay_param, "shard", axis=0, tiled=True),
        lax.all_gather(merge_weight, "shard", axis=0, tiled=True),
    )
    (
        gain_first,
        weight_branch,
        weight_gelu,
        taps_conv,
        bias_conv,
        weight_gates,
        bias_gates,
        decay_all,
        weight_merge,
    ) = block_parts
    adapter_parts = (
        lax.all_gather(down_branch, "shard", axis=1, tiled=True),
        lax.all_gather(up_branch, "shard", axis=0, tiled=True),
        lax.all_gather(down_gelu, "shard", axis=1, tiled=True),
        lax.all_gather(up_gelu, "shard", axis=0, tiled=True),
        lax.all_gather(down_gates, "shard", axis=1, tiled=True),
        lax.all_gather(up_gates, "shard", axis=0, tiled=True),
        lax.all_gather(down_merge, "shard", axis=1, tiled=True),
        lax.all_gather(up_merge, "shard", axis=0, tiled=True),
        lax.all_gather(down_feed_gate, "shard", axis=1, tiled=True),
        lax.all_gather(up_feed_gate, "shard", axis=0, tiled=True),
        lax.all_gather(down_feed_up, "shard", axis=1, tiled=True),
        lax.all_gather(up_feed_up, "shard", axis=0, tiled=True),
        lax.all_gather(down_feed_down, "shard", axis=1, tiled=True),
        lax.all_gather(up_feed_down, "shard", axis=0, tiled=True),
    )
    (
        fact_down_branch,
        fact_up_branch,
        fact_down_gelu,
        fact_up_gelu,
        fact_down_gates,
        fact_up_gates,
        fact_down_merge,
        fact_up_merge,
        fact_down_fgate,
        fact_up_fgate,
        fact_down_fup,
        fact_up_fup,
        fact_down_fdown,
        fact_up_fdown,
    ) = adapter_parts
    position, live_rows, adapter_mask = layout(seq_lengths[0], adapter_index[0], rows_here)

    def adapter_forward(act, down, up):
        rank_part = (matmul(act, down) * adapter_mask).astype(jnp.bfloat16)
        return (rank_part, matmul(rank_part, up))

    def adapter_backward(grad_low, act, rank_part, up):
        grad_rank = (matmul_right_t(grad_low, up) * adapter_mask).astype(jnp.bfloat16)
        return (grad_rank, matmul_left_t(act, grad_rank), matmul_left_t(rank_part, grad_low))

    gain_first_f = gain_first.astype(jnp.float32)
    rows_in = work_in.astype(jnp.float32)
    normed_first, first_pull = jax.vjp(lambda values: root_norm(values, gain_first_f), rows_in)
    act_first = normed_first.astype(jnp.bfloat16)
    rank_branch, extra_branch = adapter_forward(act_first, fact_down_branch, fact_up_branch)
    branch = matmul(act_first, weight_branch) + extra_branch
    rank_gelu, extra_gelu = adapter_forward(act_first, fact_down_gelu, fact_up_gelu)
    gelu_in = matmul(act_first, weight_gelu) + extra_gelu
    taps_f = taps_conv.astype(jnp.float32)
    bias_f = bias_conv.astype(jnp.float32)
    conv_out, conv_pull = jax.vjp(
        lambda values: conv_apply(values, taps_f, bias_f, position), branch
    )
    conv_low = conv_out.astype(jnp.bfloat16)
    heads = conv_low.reshape(rows_here, H, DH)
    blockwise = jnp.einsum(
        "thd,hde->the", heads, weight_gates, preferred_element_type=jnp.float32
    ).reshape(rows_here, 2 * H * DH)
    rank_gates, extra_gates = adapter_forward(conv_low, fact_down_gates, fact_up_gates)
    gate_logits = blockwise + bias_gates.astype(jnp.float32).reshape(-1)[None, :] + extra_gates
    decay_f = decay_all.astype(jnp.float32)
    mixed, mixed_pull = jax.vjp(
        lambda logits, conv_in, gelu_part: recurrence(
            logits, conv_in, gelu_part, decay_f, position
        ),
        gate_logits,
        conv_out,
        gelu_in,
    )
    mixed_low = mixed.astype(jnp.bfloat16)
    rank_merge, extra_merge = adapter_forward(mixed_low, fact_down_merge, fact_up_merge)
    resid = rows_in + matmul(mixed_low, weight_merge) + extra_merge
    feed_parts = (
        lax.all_gather(norm_second, "shard", axis=0, tiled=True),
        lax.all_gather(feed_gate, "shard", axis=1, tiled=True),
        lax.all_gather(feed_up, "shard", axis=1, tiled=True),
        lax.all_gather(feed_down, "shard", axis=0, tiled=True),
    )
    gain_second, weight_fgate, weight_fup, weight_fdown = feed_parts
    gain_second_f = gain_second.astype(jnp.float32)
    normed_second, second_pull = jax.vjp(lambda values: root_norm(values, gain_second_f), resid)
    act_second = normed_second.astype(jnp.bfloat16)
    rank_fgate, extra_fgate = adapter_forward(act_second, fact_down_fgate, fact_up_fgate)
    hidden_gate = matmul(act_second, weight_fgate) + extra_fgate
    rank_fup, extra_fup = adapter_forward(act_second, fact_down_fup, fact_up_fup)
    hidden_up = matmul(act_second, weight_fup) + extra_fup
    hidden, hidden_pull = jax.vjp(feed_mix, hidden_gate, hidden_up)
    hidden_low = hidden.astype(jnp.bfloat16)
    rank_fdown, extra_fdown = adapter_forward(hidden_low, fact_down_fdown, fact_up_fdown)
    work_out = (resid + matmul(hidden_low, weight_fdown) + extra_fdown) * live_rows[:, None]
    grad_out = work_cot.astype(jnp.float32) * live_rows[:, None]
    grad_out_low = grad_out.astype(jnp.bfloat16)
    grad_rank_fdown, grad_down_fdown, grad_up_fdown = adapter_backward(
        grad_out_low, hidden_low, rank_fdown, fact_up_fdown
    )
    grad_hidden = matmul_right_t(grad_out_low, weight_fdown) + matmul_right_t(
        grad_rank_fdown, fact_down_fdown
    )
    grad_hgate, grad_hup = hidden_pull(grad_hidden)
    grad_hgate_low = grad_hgate.astype(jnp.bfloat16)
    grad_hup_low = grad_hup.astype(jnp.bfloat16)
    grad_rank_fgate, grad_down_fgate, grad_up_fgate = adapter_backward(
        grad_hgate_low, act_second, rank_fgate, fact_up_fgate
    )
    grad_rank_fup, grad_down_fup, grad_up_fup = adapter_backward(
        grad_hup_low, act_second, rank_fup, fact_up_fup
    )
    grad_second = (
        matmul_right_t(grad_hgate_low, weight_fgate)
        + matmul_right_t(grad_hup_low, weight_fup)
        + matmul_right_t(grad_rank_fgate, fact_down_fgate)
        + matmul_right_t(grad_rank_fup, fact_down_fup)
    )
    grad_resid = grad_out + second_pull(grad_second)[0]
    grad_resid_low = grad_resid.astype(jnp.bfloat16)
    grad_rank_merge, grad_down_merge, grad_up_merge = adapter_backward(
        grad_resid_low, mixed_low, rank_merge, fact_up_merge
    )
    grad_mixed = matmul_right_t(grad_resid_low, weight_merge) + matmul_right_t(
        grad_rank_merge, fact_down_merge
    )
    grad_logits, grad_conv_direct, grad_gelu_in = mixed_pull(grad_mixed)
    grad_logits_low = grad_logits.astype(jnp.bfloat16)
    grad_rank_gates, grad_down_gates, grad_up_gates = adapter_backward(
        grad_logits_low, conv_low, rank_gates, fact_up_gates
    )
    grad_heads = jnp.einsum(
        "the,hde->thd",
        grad_logits_low.reshape(rows_here, H, 2 * DH),
        weight_gates,
        preferred_element_type=jnp.float32,
    ).reshape(rows_here, H * DH)
    grad_conv = grad_conv_direct + grad_heads + matmul_right_t(grad_rank_gates, fact_down_gates)
    grad_branch = conv_pull(grad_conv)[0]
    grad_branch_low = grad_branch.astype(jnp.bfloat16)
    grad_gelu_low = grad_gelu_in.astype(jnp.bfloat16)
    grad_rank_branch, grad_down_branch, grad_up_branch = adapter_backward(
        grad_branch_low, act_first, rank_branch, fact_up_branch
    )
    grad_rank_gelu, grad_down_gelu, grad_up_gelu = adapter_backward(
        grad_gelu_low, act_first, rank_gelu, fact_up_gelu
    )
    grad_first = (
        matmul_right_t(grad_branch_low, weight_branch)
        + matmul_right_t(grad_gelu_low, weight_gelu)
        + matmul_right_t(grad_rank_branch, fact_down_branch)
        + matmul_right_t(grad_rank_gelu, fact_down_gelu)
    )
    grad_work = grad_resid + first_pull(grad_first)[0]
    collected = (
        lax.all_gather(work_out, "shard", axis=0, tiled=True),
        lax.all_gather(grad_work, "shard", axis=0, tiled=True),
    )
    inverse = (
        jnp.zeros((group_rows,), jnp.int32)
        .at[deal_row]
        .set(jnp.arange(group_rows, dtype=jnp.int32))
    )
    my_rows = lax.dynamic_slice_in_dim(inverse, my_index * rows_here, rows_here)
    layer_out = jnp.take(collected[0], my_rows, axis=0)
    grad_tokens = jnp.take(collected[1], my_rows, axis=0)
    part_width = grad_down_branch.shape[1] // shards
    summed = lax.psum(
        (
            grad_down_branch,
            grad_up_branch,
            grad_down_gelu,
            grad_up_gelu,
            grad_down_gates,
            grad_up_gates,
            grad_down_merge,
            grad_up_merge,
            grad_down_fgate,
            grad_up_fgate,
            grad_down_fup,
            grad_up_fup,
            grad_down_fdown,
            grad_up_fdown,
        ),
        ("rep", "shard"),
    )
    owned = tuple(
        (
            lax.dynamic_slice_in_dim(
                summed[number], my_index * part_width, part_width, 1 - number % 2
            )
            for number in range(14)
        )
    )
    return (
        layer_out,
        grad_tokens,
        owned[0],
        owned[1],
        owned[2],
        owned[3],
        owned[4],
        owned[5],
        owned[6],
        owned[7],
        owned[8],
        owned[9],
        owned[10],
        owned[11],
        owned[12],
        owned[13],
    )


def solution(mesh):
    in_specs = (
        P(("rep", "shard"), None),
        P(("rep", "shard"), None),
        P("shard"),
        P(None, "shard"),
        P(None, "shard"),
        P(None, "shard"),
        P("shard"),
        P("shard", None, None),
        P("shard", None),
        P("shard"),
        P("shard", None),
        P("shard"),
        P(None, "shard"),
        P(None, "shard"),
        P("shard", None),
        P(None, "shard"),
        P("shard", None),
        P(None, "shard"),
        P("shard", None),
        P(None, "shard"),
        P("shard", None),
        P(None, "shard"),
        P("shard", None),
        P(None, "shard"),
        P("shard", None),
        P(None, "shard"),
        P("shard", None),
        P(None, "shard"),
        P("shard", None),
        P(("rep", "shard"), None),
        P(("rep", "shard"), None),
        P("rep", None),
    )
    out_specs = (
        P(("rep", "shard"), None),
        P(("rep", "shard"), None),
        P(None, "shard"),
        P("shard", None),
        P(None, "shard"),
        P("shard", None),
        P(None, "shard"),
        P("shard", None),
        P(None, "shard"),
        P("shard", None),
        P(None, "shard"),
        P("shard", None),
        P(None, "shard"),
        P("shard", None),
        P(None, "shard"),
        P("shard", None),
    )
    return jax.shard_map(local, mesh=mesh, in_specs=in_specs, out_specs=out_specs, check_vma=False)
```

profile of v0, /device:TPU:0, one launch (start us, length us, event | category | flops | bytes accessed | tf_op | source)
XLA Modules:
  0.0 3010.1 jit_solution(17063541124897532782)
XLA Ops:
  19.0 15.6 all-gather.1
  35.0 17.7 all_gather.98
  52.7 23.4 all_gather.99
  76.9 16.7 all_gather.95
  93.6 14.6 all-gather
  108.3 20.1 all_gather.102
  128.4 15.4 all-gather.2
  143.8 12.0 all-gather.3
  156.5 17.4 all_gather.106
  173.8 23.5 all_gather.107
  197.3 24.9 all_gather.109
  222.2 22.7 all_gather.110
  244.9 12.1 all-gather.4
  257.6 20.9 all_gather.116
  278.5 22.2 all_gather.113
  300.7 15.2 all_gather.120
  347.6 8.9 copy.113
  362.9 8.3 add_add_fusion
  371.1 9.3 copy.142
  398.1 11.7 exponential_select_fusion
  409.8 9.8 slice.325
  419.6 9.8 slice.326
  429.5 9.8 slice.324
  439.3 9.8 slice.328
  556.3 10.1 slice.323
  566.5 10.1 slice.388
  598.7 8.7 pad.364
  616.3 16.5 pad.367
  638.7 16.5 pad.366
  678.3 31.0 %all-gather.47.cloned.1.call-done = bf16[2048,1536]{1,0:T(8,128)(2,1)} async-done(((bf16[512,1536]{1,0:T(8,128)(2,1)}), bf16[2048,1536]{1,0:T(8,128)(2,1)}) %all-gather.47.cloned.1.call-update) | async-done | bytes 6291472 | tf_op jit(solution)/shard_map/all_gather | solution.py:127
  709.3 8.2 gather_fusion.2
  720.0 233.1 %all-gather.37.cloned.1.call-done = bf16[1536,4608]{1,0:T(8,128)(2,1)} async-done(((bf16[1536,1152]{1,0:T(8,128)(2,1)}), bf16[1536,4608]{1,0:T(8,128)(2,1)}) %all-gather.37.cloned.1.call-update) | async-done | bytes 14155792 | tf_op jit(solution)/shard_map/all_gather | solution.py:231
  953.1 12.9 fusion.130
  965.9 230.9 %all-gather.33.cloned.1.call-done = bf16[1536,4608]{1,0:T(8,128)(2,1)} async-done(((bf16[1536,1152]{1,0:T(8,128)(2,1)}), bf16[1536,4608]{1,0:T(8,128)(2,1)}) %all-gather.33.cloned.1.call-update) | async-done | bytes 14155792 | tf_op jit(solution)/shard_map/all_gather | solution.py:230
  1196.8 12.8 fusion.129
  1209.7 17.2 all-gather.39.cloned.1.call-done
  1226.9 9.0 convolution_add_fusion.1
  1235.9 22.2 all-gather.35.cloned.1.call-done
  1258.1 10.0 convolution_add_fusion.2
  1268.1 234.5 %all-gather.41.cloned.1.call-done = bf16[4608,1536]{1,0:T(8,128)(2,1)} async-done(((bf16[1152,1536]{1,0:T(8,128)(2,1)}), bf16[4608,1536]{1,0:T(8,128)(2,1)}) %all-gather.41.cloned.1.call-update) | async-done | bytes 14155792 | tf_op jit(solution)/shard_map/all_gather | solution.py:232
  1502.6 13.4 fusion.95
  1516.0 16.8 all-gather.43.cloned.1.call-done
  1532.8 17.3 multiply_convert_fusion
  1550.1 13.4 fusion.131
  1564.9 10.3 convolution_add_fusion.12
  1598.4 9.8 slice.389
  1615.1 9.8 slice.390
  1714.0 8.8 pad.425
  1727.5 8.6 pad.450
  1736.2 8.7 pad.375
  1749.8 11.2 multiply_add_fusion.1
  1763.9 16.6 pad.426
  1780.5 16.5 pad.427
  1797.0 16.6 pad.451
  1813.6 16.6 pad.452
  1830.2 16.9 pad.370
  1847.1 16.9 pad.428
  1864.0 18.5 multiply_multiply_fusion.5
  1977.3 12.4 convolution_add_fusion.13
  2019.8 528.0 %all-reduce.96.cloned.1.call-done = (f32[1536,128]{0,1:T(8,128)}, f32[128,2048]{1,0:T(8,128)}, f32[1536,128]{0,1:T(8,128)}, f32[128,2048]{1,0:T(8,128)}, f32[204...) async-done(((f32[1536,128]{0,1:T(8,128)}, ...) | async-done | bytes 18087952 | tf_op jit(solution)/shard_map/psum | solution.py:318
  2563.3 207.1 %all-gather.45.cloned.1.call-done = f32[2048,1536]{1,0:T(8,128)} async-done(((f32[512,1536]{1,0:T(8,128)}), f32[2048,1536]{1,0:T(8,128)}) %all-gather.45.cloned.1.call-update) | async-done | bytes 12582928 | tf_op jit(solution)/shard_map/all_gather | solution.py:306
  2770.3 8.3 gather_fusion.1
  2778.6 210.2 %all-gather.49.cloned.1.call-done = f32[2048,1536]{1,0:T(8,128)} async-done(((f32[512,1536]{1,0:T(8,128)}), f32[2048,1536]{1,0:T(8,128)}) %all-gather.49.cloned.1.call-update) | async-done | bytes 12582928 | tf_op jit(solution)/shard_map/all_gather | solution.py:307
  2988.8 9.1 gather_fusion.3
  (797 shorter events, 515.4 us)
Async XLA Ops:
  7.2 310.7 %all-gather.21.cloned.1.call-start = ((), (), s32[]{:S(2)}) async-start(), calls=%async_computation | async-start | bytes 7864320 | tf_op jit(solution)/shard_map/all_gather | solution.py:126
  7.9 321.1 %all-gather.23.cloned.1.call-start = ((), (), s32[]{:S(2)}) async-start(), calls=%async_computation.1 | async-start | bytes 7864320 | tf_op jit(solution)/shard_map/all_gather | solution.py:134
  8.7 332.4 %all-gather.25.cloned.1.call-start = ((), (), s32[]{:S(2)}) async-start(), calls=%async_computation.2 | async-start | bytes 1310720 | tf_op jit(solution)/shard_map/all_gather | solution.py:138
  9.4 353.5 %all-gather.27.cloned.1.call-start = ((), (), s32[]{:S(2)}) async-start(), calls=%async_computation.3 | async-start | bytes 1310720 | tf_op jit(solution)/shard_map/all_gather | solution.py:160
  10.0 645.9 %all-gather.29.cloned.1.call-start = ((), (), s32[]{:S(2)}) async-start(), calls=%async_computation.4 | async-start | bytes 7864320 | tf_op jit(solution)/shard_map/all_gather | solution.py:135
  10.6 657.5 %all-gather.31.cloned.1.call-start = ((), (), s32[]{:S(2)}) async-start(), calls=%async_computation.5 | async-start | bytes 7864320 | tf_op jit(solution)/shard_map/all_gather | solution.py:141
  11.1 698.2 %all-gather.47.cloned.1.call-start = ((), (), s32[]{:S(2)}) async-start(), calls=%async_computation.13 | async-start | bytes 7864320 | tf_op jit(solution)/shard_map/all_gather | solution.py:127
  11.9 941.2 %all-gather.37.cloned.1.call-start = ((), (), s32[]{:S(2)}) async-start(), calls=%async_computation.8 | async-start | bytes 17694720 | tf_op jit(solution)/shard_map/all_gather | solution.py:231
  12.7 22.1 copy-start.211
  12.7 22.3 copy-start.168
  12.7 40.0 %copy-start.157 = (bf16[32,2048]{1,0:T(8,128)(2,1)S(1)}, bf16[32,2048]{1,0:T(8,128)(2,1)}, u32[]{:S(2)}) copy-start(bf16[32,2048]{1,0:T(8,128)(2,1)} %param.52) | copy-start | bytes 393220
  12.7 64.2 %copy-start.204 = (bf16[4,512]{1,0:T(4,128)(2,1)S(1)}, bf16[4,512]{1,0:T(4,128)(2,1)}, u32[]{:S(2)}) copy-start(bf16[4,512]{1,0:T(4,128)(2,1)} %param.41) | copy-start | bytes 12292
  12.7 80.9 %copy-start.206 = (bf16[512]{0:T(512)(128)(2,1)S(1)}, bf16[512]{0:T(512)(128)(2,1)}, u32[]{:S(2)}) copy-start(bf16[512]{0:T(512)(128)(2,1)} %param.42) | copy-start | bytes 3076
  12.7 1184.1 %all-gather.33.cloned.1.call-start = ((), (), s32[]{:S(2)}) async-start(), calls=%async_computation.6 | async-start | bytes 17694720 | tf_op jit(solution)/shard_map/all_gather | solution.py:230
  13.4 94.8 %copy-start.158 = (bf16[2048,32]{0,1:T(8,128)(2,1)S(1)}, bf16[2048,32]{0,1:T(8,128)(2,1)}, u32[]{:S(2)}) copy-start(bf16[2048,32]{0,1:T(8,128)(2,1)} %param.55) | copy-start | bytes 393220
  13.5 114.9 %copy-start.205 = (bf16[4,256]{1,0:T(4,128)(2,1)S(1)}, bf16[4,256]{1,0:T(4,128)(2,1)}, u32[]{:S(2)}) copy-start(bf16[4,256]{1,0:T(4,128)(2,1)} %param.44) | copy-start | bytes 6148
  13.5 130.4 %copy-start.207 = (bf16[512]{0:T(512)(128)(2,1)S(1)}, bf16[512]{0:T(512)(128)(2,1)}, u32[]{:S(2)}) copy-start(bf16[512]{0:T(512)(128)(2,1)} %param.45) | copy-start | bytes 3076
  13.5 143.0 %copy-start.169 = (bf16[1536,32]{0,1:T(8,128)(2,1)S(1)}, bf16[1536,32]{0,1:T(8,128)(2,1)}, u32[]{:S(2)}) copy-start(bf16[1536,32]{0,1:T(8,128)(2,1)} %param.53) | copy-start | bytes 294916
  13.5 160.3 %copy-start.159 = (bf16[32,2048]{1,0:T(8,128)(2,1)S(1)}, bf16[32,2048]{1,0:T(8,128)(2,1)}, u32[]{:S(2)}) copy-start(bf16[32,2048]{1,0:T(8,128)(2,1)} %param.54) | copy-start | bytes 393220
  13.5 1213.4 %all-gather.39.cloned.1.call-start = ((), (), s32[]{:S(2)}) async-start(), calls=%async_computation.9 | async-start | bytes 1474560 | tf_op jit(solution)/shard_map/all_gather | solution.py:166
  14.1 183.2 %copy-start.160 = (bf16[2048,32]{0,1:T(8,128)(2,1)S(1)}, bf16[2048,32]{0,1:T(8,128)(2,1)}, u32[]{:S(2)}) copy-start(bf16[2048,32]{0,1:T(8,128)(2,1)} %param.57) | copy-start | bytes 393220
  14.1 1244.0 %all-gather.35.cloned.1.call-start = ((), (), s32[]{:S(2)}) async-start(), calls=%async_computation.7 | async-start | bytes 1474560 | tf_op jit(solution)/shard_map/all_gather | solution.py:164
  14.8 207.3 %copy-start.170 = (bf16[32,1536]{1,0:T(8,128)(2,1)S(1)}, bf16[32,1536]{1,0:T(8,128)(2,1)}, u32[]{:S(2)}) copy-start(bf16[32,1536]{1,0:T(8,128)(2,1)} %param.58) | copy-start | bytes 294916
  14.8 230.0 %copy-start.209 = (bf16[384]{0:T(512)(128)(2,1)S(1)}, bf16[384]{0:T(512)(128)(2,1)}, u32[]{:S(2)}) copy-start(bf16[384]{0:T(512)(128)(2,1)} %param.47) | copy-start | bytes 2308
  14.9 242.7 %copy-start.171 = (bf16[1536,32]{0,1:T(8,128)(2,1)S(1)}, bf16[1536,32]{0,1:T(8,128)(2,1)}, u32[]{:S(2)}) copy-start(bf16[1536,32]{0,1:T(8,128)(2,1)} %param.61) | copy-start | bytes 294916
  14.9 263.6 %copy-start.172 = (bf16[1536,32]{0,1:T(8,128)(2,1)S(1)}, bf16[1536,32]{0,1:T(8,128)(2,1)}, u32[]{:S(2)}) copy-start(bf16[1536,32]{0,1:T(8,128)(2,1)} %param.59) | copy-start | bytes 294916
  14.9 285.8 %copy-start.173 = (bf16[32,1536]{1,0:T(8,128)(2,1)S(1)}, bf16[32,1536]{1,0:T(8,128)(2,1)}, u32[]{:S(2)}) copy-start(bf16[32,1536]{1,0:T(8,128)(2,1)} %param.64) | copy-start | bytes 294916
  14.9 1487.7 %all-gather.41.cloned.1.call-start = ((), (), s32[]{:S(2)}) async-start(), calls=%async_computation.10 | async-start | bytes 17694720 | tf_op jit(solution)/shard_map/all_gather | solution.py:232
  15.5 1517.3 %all-gather.43.cloned.1.call-start = ((), (), s32[]{:S(2)}) async-start(), calls=%async_computation.11 | async-start | bytes 1474560 | tf_op jit(solution)/shard_map/all_gather | solution.py:167
  16.2 2531.6 %all-reduce.96.cloned.1.call-start = ((), (), s32[]{:S(2)}) async-start(), calls=%async_computation.15 | async-start | bytes 36175872 | tf_op jit(solution)/shard_map/psum | solution.py:318
  34.7 291.6 %copy-start.177 = (f32[1536]{0:T(1024)}, f32[1536]{0:T(1024)S(1)}, u32[]{:S(2)}) copy-start(f32[1536]{0:T(1024)S(1)} %reshape.246) | copy-start | bytes 18436
  52.7 275.7 %copy-start.72 = (bf16[1536,128]{0,1:T(8,128)(2,1)}, bf16[1536,128]{0,1:T(8,128)(2,1)S(1)}, u32[]{:S(2)}) copy-start(bf16[1536,128]{0,1:T(8,128)(2,1)S(1)} %all_gather.98) | copy-start | bytes 1179652
  76.0 258.5 %copy-start.49 = (bf16[128,2048]{1,0:T(8,128)(2,1)}, bf16[128,2048]{1,0:T(8,128)(2,1)S(1)}, u32[]{:S(2)}) copy-start(bf16[128,2048]{1,0:T(8,128)(2,1)S(1)} %all_gather.99) | copy-start | bytes 1572868
  76.8 321.3 %copy-start.198 = (pred[512]{0:T(512)(128)(4,1)}, pred[512]{0:T(512)(128)(4,1)S(1)}, u32[]{:S(2)}) copy-start(pred[512]{0:T(512)(128)(4,1)S(1)} %get-tuple-element.146) | copy-start | bytes 1540
  93.6 241.7 %copy-start.175 = (f32[1,2048]{1,0:T(1,128)}, f32[1,2048]{1,0:T(1,128)S(1)}, u32[]{:S(2)}) copy-start(f32[1,2048]{1,0:T(1,128)S(1)} %get-tuple-element.140) | copy-start | bytes 24580
  93.6 241.7 %copy-start.179 = (f32[1,2048]{1,0:T(1,128)}, f32[1,2048]{1,0:T(1,128)S(1)}, u32[]{:S(2)}) copy-start(f32[1,2048]{1,0:T(1,128)S(1)} %get-tuple-element.141) | copy-start | bytes 24580
  93.6 241.7 %copy-start.181 = (f32[1,2048]{1,0:T(1,128)}, f32[1,2048]{1,0:T(1,128)S(1)}, u32[]{:S(2)}) copy-start(f32[1,2048]{1,0:T(1,128)S(1)} %get-tuple-element.143) | copy-start | bytes 24580
  93.6 241.7 %copy-start.183 = (f32[1,2048]{1,0:T(1,128)}, f32[1,2048]{1,0:T(1,128)S(1)}, u32[]{:S(2)}) copy-start(f32[1,2048]{1,0:T(1,128)S(1)} %get-tuple-element.142) | copy-start | bytes 24580
  128.3 228.2 %copy-start.46 = (bf16[2048,128]{0,1:T(8,128)(2,1)}, bf16[2048,128]{0,1:T(8,128)(2,1)S(1)}, u32[]{:S(2)}) copy-start(bf16[2048,128]{0,1:T(8,128)(2,1)S(1)} %all_gather.102) | copy-start | bytes 1572868
  156.5 241.7 %copy-start.151 = (f32[2048]{0:T(1024)}, f32[2048]{0:T(1024)S(1)}, u32[]{:S(2)}) copy-start(f32[2048]{0:T(1024)S(1)} %get-tuple-element.145) | copy-start | bytes 24580
  328.4 327.5 %copy-start.12 = (bf16[512,1536]{1,0:T(8,128)(2,1)}, bf16[512,1536]{1,0:T(8,128)(2,1)S(1)}, u32[]{:S(2)}) copy-start(bf16[512,1536]{1,0:T(8,128)(2,1)S(1)} %fusion.33) | copy-start | bytes 4718596
  497.8 41.8 %copy-start.62 = (f32[32,2048]{1,0:T(8,128)}, f32[32,2048]{1,0:T(8,128)S(1)}, u32[]{:S(2)}) copy-start(f32[32,2048]{1,0:T(8,128)S(1)} %slice.342) | copy-start | bytes 786436
  501.5 33.2 %copy-start.76 = (f32[64,2048]{1,0:T(8,128)S(1)}, f32[64,2048]{1,0:T(8,128)}, u32[]{:S(2)}) copy-start(f32[64,2048]{1,0:T(8,128)} %get-tuple-element.95) | copy-start | bytes 1572868
  502.6 47.3 %copy-start.111 = (f32[16,2048]{1,0:T(8,128)}, f32[16,2048]{1,0:T(8,128)S(1)}, u32[]{:S(2)}) copy-start(f32[16,2048]{1,0:T(8,128)S(1)} %slice.349) | copy-start | bytes 393220
  505.2 44.6 %copy-start.88 = (f32[16,2048]{1,0:T(8,128)}, f32[16,2048]{1,0:T(8,128)S(1)}, u32[]{:S(2)}) copy-start(f32[16,2048]{1,0:T(8,128)S(1)} %slice.348) | copy-start | bytes 393220
  506.3 43.6 %copy-start.113 = (f32[16,2048]{1,0:T(8,128)}, f32[16,2048]{1,0:T(8,128)S(1)}, u32[]{:S(2)}) copy-start(f32[16,2048]{1,0:T(8,128)S(1)} %slice.352) | copy-start | bytes 393220
  507.3 24.9 copy-start.130
  508.0 47.4 %copy-start.126 = (f32[8,2048]{1,0:T(8,128)}, f32[8,2048]{1,0:T(8,128)S(1)}, u32[]{:S(2)}) copy-start(f32[8,2048]{1,0:T(8,128)S(1)} %slice.354) | copy-start | bytes 196612
  508.1 24.1 copy-start.132
  521.7 33.7 %copy-start.162 = (f32[1,2048]{1,0:T(1,128)}, f32[1,2048]{1,0:T(1,128)S(1)}, u32[]{:S(2)}) copy-start(f32[1,2048]{1,0:T(1,128)S(1)} %get-tuple-element.138) | copy-start | bytes 24580
  528.2 50.0 %copy-start.128 = (f32[7,2048]{1,0:T(8,128)}, f32[7,2048]{1,0:T(8,128)S(1)}, u32[]{:S(2)}) copy-start(f32[7,2048]{1,0:T(8,128)S(1)} %slice.353) | copy-start | bytes 172036
  530.5 48.5 %copy-start.109 = (f32[15,2048]{1,0:T(8,128)}, f32[15,2048]{1,0:T(8,128)S(1)}, u32[]{:S(2)}) copy-start(f32[15,2048]{1,0:T(8,128)S(1)} %slice.347) | copy-start | bytes 368644
  534.8 45.7 %copy-start.77 = (f32[31,2048]{1,0:T(8,128)}, f32[31,2048]{1,0:T(8,128)S(1)}, u32[]{:S(2)}) copy-start(f32[31,2048]{1,0:T(8,128)S(1)} %slice.341) | copy-start | bytes 761860
  556.3 21.9 copy-start.190
  677.1 519.7 %copy-start.14 = (bf16[512,1536]{1,0:T(8,128)(2,1)}, bf16[512,1536]{1,0:T(8,128)(2,1)S(1)}, u32[]{:S(2)}) copy-start(bf16[512,1536]{1,0:T(8,128)(2,1)S(1)} %multiply_convert_fusion.3) | copy-start | bytes 4718596
  677.7 549.2 %copy-start.92 = (bf16[512,128]{1,0:T(8,128)(2,1)}, bf16[512,128]{1,0:T(8,128)(2,1)S(1)}, u32[]{:S(2)}) copy-start(bf16[512,128]{1,0:T(8,128)(2,1)S(1)} %fusion.49) | copy-start | bytes 393220
  678.3 579.7 %copy-start.94 = (bf16[512,128]{1,0:T(8,128)(2,1)}, bf16[512,128]{1,0:T(8,128)(2,1)S(1)}, u32[]{:S(2)}) copy-start(bf16[512,128]{1,0:T(8,128)(2,1)S(1)} %fusion.48) | copy-start | bytes 393220
  720.0 812.8 %copy-start.155 = (bf16[512,128]{1,0:T(8,128)(2,1)}, bf16[512,128]{1,0:T(8,128)(2,1)S(1)}, u32[]{:S(2)}) copy-start(bf16[512,128]{1,0:T(8,128)(2,1)S(1)} %fusion.50) | copy-start | bytes 393220
  1235.9 266.7 %copy-start.42 = (bf16[512,1536]{1,0:T(8,128)(2,1)S(1)}, bf16[512,1536]{1,0:T(8,128)(2,1)}, u32[]{:S(2)}) copy-start(bf16[512,1536]{1,0:T(8,128)(2,1)} %gather_fusion.2) | copy-start | bytes 4718596
  1550.1 25.8 copy-start.25
  1722.8 22.1 copy-start.60
  1727.5 22.2 slice-start.7
  1975.4 794.9 %all-gather.45.cloned.1.call-start = ((), (), s32[]{:S(2)}) async-start(), calls=%async_computation.12 | async-start | bytes 15728640 | tf_op jit(solution)/shard_map/all_gather | solution.py:306
  1992.8 996.1 %all-gather.49.cloned.1.call-start = ((), (), s32[]{:S(2)}) async-start(), calls=%async_computation.14 | async-start | bytes 15728640 | tf_op jit(solution)/shard_map/all_gather | solution.py:307
  (177 other events, 1174.7 us)
Sparse Core Ops, SparseCore 0:
  9.6 143.8 all-gather.20
  155.0 150.7 all-gather.22
  307.4 26.5 all-gather.24
  335.4 27.4 all-gather.26
  364.3 114.8 all-gather.28
  480.6 113.5 all-gather.30
  595.7 113.5 all-gather.46
  710.9 242.1 all-gather.36
  954.7 242.1 all-gather.32
  1198.2 28.6 all-gather.38
  1228.5 29.5 all-gather.34
  1259.5 243.0 all-gather.40
  1504.1 28.6 all-gather.42
  1975.5 572.2 all-reduce.95
  2550.8 219.4 all-gather.44
  2772.4 216.3 all-gather.48
where the time goes:
time: 3020 us; the launch traced here: 3010 us
  waiting for transfers between devices  1740 us (58%)
  local copies, waits for them, and re-layouts  543 us (18%)
  blocking collectives  294 us (10%)
  matrix products  234 us (8%)
  other arithmetic  177 us (6%)
    psum x1, waiting for transfers between devices, local(): lax.psum((grad_down_branch, grad_up_branch, grad_down_gelu, grad_up_gelu,...  528 us
    pad x70, local copies, waits for them, and re-layouts, recurrence(): unused, state = lax.associative_scan(combine, (carried, driven), axis=0)  244 us
    all_gather x1, waiting for transfers between devices, local(): lax.all_gather(feed_down, 'shard', axis=0, tiled=True)  234 us
    all_gather x1, waiting for transfers between devices, local(): lax.all_gather(feed_up, 'shard', axis=1, tiled=True)  233 us
    all_gather x1, waiting for transfers between devices, local(): lax.all_gather(feed_gate, 'shard', axis=1, tiled=True)  231 us
    all_gather x1, waiting for transfers between devices, local(): lax.all_gather(grad_work, 'shard', axis=0, tiled=True)  210 us
    all_gather x1, waiting for transfers between devices, local(): lax.all_gather(work_out, 'shard', axis=0, tiled=True)  207 us
    slice x69, local copies, waits for them, and re-layouts, recurrence(): unused, state = lax.associative_scan(combine, (carried, driven), axis=0)  178 us
  transfers between devices with their start and end apart: 16, of which 11 were waited for; matrix products, arithmetic and copies ran while one was open for 16% of the time, Pallas kernels for 0%

commit v1 on v0

--- a/solution.py
+++ b/solution.py
@@ -117,6 +117,24 @@
     adapter_index,
     deal_order,
 ):
+
+    def open_the_grid(xx, row_axis, d0):
+        w_next = lax.axis_size(row_axis)
+        upper = lax.axis_index(row_axis)
+        r_now, mat_out, arr_out = (w_next, upper, xx.shape[d0])
+        inter, base_arr = (xx, 1)
+        while base_arr < r_now:
+            row_list = []
+            num = 0
+            while num < r_now:
+                row_list.append((num, (num - base_arr) % r_now))
+                num = num + 1
+            clean = lax.ppermute(inter, row_axis, row_list)
+            inter = jnp.concatenate([inter, clean], d0)
+            base_arr = 2 * base_arr
+        aux = jnp.roll(inter, mat_out * arr_out, d0)
+        return aux
+
     rows_here = tokens.shape[0]
     shards = lax.axis_size("shard")
     my_index = lax.axis_index("shard")
@@ -227,7 +245,7 @@
     resid = rows_in + matmul(mixed_low, weight_merge) + extra_merge
     feed_parts = (
         lax.all_gather(norm_second, "shard", axis=0, tiled=True),
-        lax.all_gather(feed_gate, "shard", axis=1, tiled=True),
+        open_the_grid(feed_gate, row_axis="shard", d0=1),
         lax.all_gather(feed_up, "shard", axis=1, tiled=True),
         lax.all_gather(feed_down, "shard", axis=0, tiled=True),
     )

time: 3020 us -> 3130 us (1.036)
  blocking collectives: 294 us -> 446 us
  waiting for transfers between devices: 1740 us -> 1600 us
  local copies, waits for them, and re-layouts: 543 us -> 594 us
    all_gather x1 -> x0, waiting for transfers between devices: 231 us -> none  [local(): lax.all_gather(feed_gate, 'shard', axis=1, tiled=True)]
    all_gather x1, blocking collectives: 15.6 us -> 179 us  [local(): lax.all_gather(norm_first, 'shard', axis=0, tiled=True)]
    all_gather x1, waiting for transfers between devices: 0.02 us -> 138 us  [local(): lax.all_gather(merge_weight, 'shard', axis=0, tiled=True)]
  transfers between devices with their start and end apart: 16 -> 17, of which waited for: 11 -> 10; matrix products, arithmetic and copies ran while one was open for 16% -> 18% of each run, Pallas kernels for 0% -> 0%
where the time goes in v1:
time: 3130 us; the launch traced here: 3120 us
  waiting for transfers between devices  1600 us (51%)
  local copies, waits for them, and re-layouts  594 us (19%)
  blocking collectives  446 us (14%)
  matrix products  247 us (8%)
  other arithmetic  199 us (6%)
    psum x1, waiting for transfers between devices, local(): lax.psum((grad_down_branch, grad_up_branch, grad_down_gelu, grad_up_gelu,...  532 us
    pad x70, local copies, waits for them, and re-layouts, recurrence(): unused, state = lax.associative_scan(combine, (carried, driven), axis=0)  244 us
    all_gather x1, waiting for transfers between devices, local(): lax.all_gather(feed_up, 'shard', axis=1, tiled=True)  235 us
    all_gather x1, waiting for transfers between devices, local(): lax.all_gather(feed_down, 'shard', axis=0, tiled=True)  216 us
    all_gather x1, waiting for transfers between devices, local(): lax.all_gather(work_out, 'shard', axis=0, tiled=True)  210 us
    all_gather x1, waiting for transfers between devices, local(): lax.all_gather(grad_work, 'shard', axis=0, tiled=True)  208 us
    slice x69, local copies, waits for them, and re-layouts, recurrence(): unused, state = lax.associative_scan(combine, (carried, driven), axis=0)  199 us
    all_gather x1, blocking collectives, local(): lax.all_gather(norm_first, 'shard', axis=0, tiled=True)  179 us
  transfers between devices with their start and end apart: 17, of which 10 were waited for; matrix products, arithmetic and copies ran while one was open for 18% of the time, Pallas kernels for 0%

profile of v1, /device:TPU:0, one launch (start us, length us, event | category | flops | bytes accessed | tf_op | source)
XLA Modules:
  0.0 3116.5 jit_solution(6743763452970322956)
XLA Ops:
  23.0 178.9 %all-gather.1 = bf16[4,1,384]{2,1,0:T(2,128)(2,1)S(1)} all-gather(bf16[1,1,384]{2,1,0:T(2,128)(2,1)S(1)} %reshape.237), channel_id=1, replica_groups=mesh['rep'=8,'shard'=4] {'shard'}, dimensions={0}, use_global_device_ids=true | all-gather | bytes 3840 | tf_op jit(solution)/shard_map/all_gather | solution.py:151
  202.9 13.2 all_gather.92
  216.1 12.1 all-gather
  228.8 13.4 all-gather.2
  242.8 15.7 all-gather.3
  258.5 11.9 all-gather.4
  273.1 20.5 all_gather.95
  293.6 22.8 all_gather.103
  316.4 20.1 all_gather.107
  336.5 16.3 all_gather.116
  352.8 19.1 all_gather.112
  371.9 16.0 all_gather.109
  388.0 24.0 all_gather.96
  411.9 16.4 all_gather.99
  428.3 20.6 all_gather.104
  448.9 25.2 all_gather.106
  525.0 9.0 copy.113
  537.0 8.2 add_add_fusion
  545.2 9.1 copy.142
  571.9 11.7 exponential_select_fusion
  583.7 9.8 slice.328
  593.4 9.8 slice.324
  603.2 9.8 slice.326
  613.0 9.8 slice.325
  797.2 10.1 slice.388
  807.3 10.0 slice.323
  821.7 8.6 pad.365
  832.6 8.6 pad.364
  850.1 16.6 pad.366
  866.7 16.6 pad.367
  910.3 137.8 %all-gather.30.cloned.1.call-done = bf16[2048,1536]{1,0:T(8,128)(2,1)} async-done(((bf16[512,1536]{1,0:T(8,128)(2,1)}), bf16[2048,1536]{1,0:T(8,128)(2,1)}) %all-gather.30.cloned.1.call-update) | async-done | bytes 6291472 | tf_op jit(solution)/shard_map/all_gather | solution.py:159
  1060.1 19.7 all-gather.32.cloned.1.call-done
  1108.8 215.6 %all-gather.38.cloned.1.call-done = bf16[4608,1536]{1,0:T(8,128)(2,1)} async-done(((bf16[1152,1536]{1,0:T(8,128)(2,1)}), bf16[4608,1536]{1,0:T(8,128)(2,1)}) %all-gather.38.cloned.1.call-update) | async-done | bytes 14155792 | tf_op jit(solution)/shard_map/all_gather | solution.py:250
  1324.4 13.8 fusion.110
  1338.2 16.3 all-gather.40.cloned.1.call-done
  1354.5 9.9 convolution_add_fusion
  1364.4 234.7 %all-gather.34.cloned.1.call-done = bf16[1536,4608]{1,0:T(8,128)(2,1)} async-done(((bf16[1536,1152]{1,0:T(8,128)(2,1)}), bf16[1536,4608]{1,0:T(8,128)(2,1)}) %all-gather.34.cloned.1.call-update) | async-done | bytes 14155792 | tf_op jit(solution)/shard_map/all_gather | solution.py:249
  1599.1 13.5 fusion.145
  1612.6 16.6 all-gather.36.cloned.1.call-done
  1629.2 9.1 convolution_add_fusion.1
  1638.4 34.7 %multiply_convert_fusion = (bf16[512,4608]{1,0:T(8,128)(2,1)}, bf16[512,4608]{1,0:T(8,128)(2,1)}, bf16[512,4608]{1,0:T(8,128)(2,1)}) fusion(f32[512,4608]{1,0:T(8,128)} %convolution_add_fusion, f32[512,4608]{1,0:T(8,128)} %convolution_add_fusion.1, f32[512,4608]{1,0:T(8,128)} %fusion.144, bf16[512,1536]{1,0:T(8,128)(2,1)S(1)} %copy-done.12, ...), kind=kOutput, calls=%fused_computation.18 | convolution fusion | flops 7311458304 | bytes 58195972 | tf_op jit(solution)/shard_map/dot_general | solution.py:15
  1679.2 12.1 fusion.146
  1691.3 13.1 fusion.39
  1723.4 9.9 slice.390
  1733.3 10.2 slice.389
  1849.6 8.7 pad.449
  1858.3 8.6 pad.425
  1871.7 10.4 multiply_add_fusion.1
  1885.2 16.5 pad.426
  1901.7 16.7 pad.452
  1918.4 9.0 pad.428
  1927.3 16.6 pad.451
  1944.0 16.7 pad.427
  1960.7 9.1 pad.370
  1969.8 18.3 multiply_multiply_fusion.5
  1993.6 9.8 fusion.49
  2008.7 8.7 fusion.21
  2033.1 8.1 add_add_fusion.3
  2099.0 12.0 convolution_add_fusion.10
  2121.6 531.9 %all-reduce.96.cloned.1.call-done = (f32[1536,128]{0,1:T(8,128)}, f32[128,2048]{1,0:T(8,128)}, f32[1536,128]{0,1:T(8,128)}, f32[128,2048]{1,0:T(8,128)}, f32[204...) async-done(((f32[1536,128]{0,1:T(8,128)}, ...) | async-done | bytes 18087952 | tf_op jit(solution)/shard_map/psum | solution.py:336
  2669.0 207.6 %all-gather.46.cloned.1.call-done = f32[2048,1536]{1,0:T(8,128)} async-done(((f32[512,1536]{1,0:T(8,128)}), f32[2048,1536]{1,0:T(8,128)}) %all-gather.46.cloned.1.call-update) | async-done | bytes 12582928 | tf_op jit(solution)/shard_map/all_gather | solution.py:325
  2876.6 8.3 gather_fusion.3
  2884.9 210.2 %all-gather.42.cloned.1.call-done = f32[2048,1536]{1,0:T(8,128)} async-done(((f32[512,1536]{1,0:T(8,128)}), f32[2048,1536]{1,0:T(8,128)}) %all-gather.42.cloned.1.call-update) | async-done | bytes 12582928 | tf_op jit(solution)/shard_map/all_gather | solution.py:324
  3095.1 9.1 gather_fusion.1
  (770 shorter events, 602.5 us)
Async XLA Ops:
  7.2 488.4 %all-gather.20.cloned.1.call-start = ((), (), s32[]{:S(2)}) async-start(), calls=%async_computation | async-start | bytes 7864320 | tf_op jit(solution)/shard_map/all_gather | solution.py:144
  7.9 498.3 %all-gather.22.cloned.1.call-start = ((), (), s32[]{:S(2)}) async-start(), calls=%async_computation.1 | async-start | bytes 7864320 | tf_op jit(solution)/shard_map/all_gather | solution.py:152
  8.7 509.8 %all-gather.24.cloned.1.call-start = ((), (), s32[]{:S(2)}) async-start(), calls=%async_computation.2 | async-start | bytes 1310720 | tf_op jit(solution)/shard_map/all_gather | solution.py:156
  9.4 527.6 %all-gather.26.cloned.1.call-start = ((), (), s32[]{:S(2)}) async-start(), calls=%async_computation.3 | async-start | bytes 1310720 | tf_op jit(solution)/shard_map/all_gather | solution.py:178
  10.0 873.3 %all-gather.44.cloned.1.call-start = ((), (), s32[]{:S(2)}) async-start(), calls=%async_computation.12 | async-start | bytes 7864320 | tf_op jit(solution)/shard_map/all_gather | solution.py:145
  10.6 887.3 %all-gather.28.cloned.1.call-start = ((), (), s32[]{:S(2)}) async-start(), calls=%async_computation.4 | async-start | bytes 7864320 | tf_op jit(solution)/shard_map/all_gather | solution.py:153
  11.1 1036.9 %all-gather.30.cloned.1.call-start = ((), (), s32[]{:S(2)}) async-start(), calls=%async_computation.5 | async-start | bytes 7864320 | tf_op jit(solution)/shard_map/all_gather | solution.py:159
  11.9 190.7 %copy-start.191 = (s32[1,4]{1,0:T(1,128)S(1)}, s32[1,4]{1,0:T(1,128)}, u32[]{:S(2)}) copy-start(s32[1,4]{1,0:T(1,128)} %param.66) | copy-start | bytes 52
  11.9 1067.8 %all-gather.32.cloned.1.call-start = ((), (), s32[]{:S(2)}) async-start(), calls=%async_computation.6 | async-start | bytes 1474560 | tf_op jit(solution)/shard_map/all_gather | solution.py:182
  12.7 190.2 %copy-start.185 = (bf16[4,512]{1,0:T(4,128)(2,1)S(1)}, bf16[4,512]{1,0:T(4,128)(2,1)}, u32[]{:S(2)}) copy-start(bf16[4,512]{1,0:T(4,128)(2,1)} %param.41) | copy-start | bytes 12292
  12.7 203.4 %copy-start.187 = (bf16[512]{0:T(512)(128)(2,1)S(1)}, bf16[512]{0:T(512)(128)(2,1)}, u32[]{:S(2)}) copy-start(bf16[512]{0:T(512)(128)(2,1)} %param.42) | copy-start | bytes 3076
  12.7 216.1 %copy-start.186 = (bf16[4,256]{1,0:T(4,128)(2,1)S(1)}, bf16[4,256]{1,0:T(4,128)(2,1)}, u32[]{:S(2)}) copy-start(bf16[4,256]{1,0:T(4,128)(2,1)} %param.44) | copy-start | bytes 6148
  12.7 230.1 %copy-start.188 = (bf16[512]{0:T(512)(128)(2,1)S(1)}, bf16[512]{0:T(512)(128)(2,1)}, u32[]{:S(2)}) copy-start(bf16[512]{0:T(512)(128)(2,1)} %param.45) | copy-start | bytes 3076
  12.7 245.8 %copy-start.190 = (bf16[384]{0:T(512)(128)(2,1)S(1)}, bf16[384]{0:T(512)(128)(2,1)}, u32[]{:S(2)}) copy-start(bf16[384]{0:T(512)(128)(2,1)} %param.47) | copy-start | bytes 2308
  12.7 260.4 %copy-start.139 = (bf16[1536,32]{0,1:T(8,128)(2,1)S(1)}, bf16[1536,32]{0,1:T(8,128)(2,1)}, u32[]{:S(2)}) copy-start(bf16[1536,32]{0,1:T(8,128)(2,1)} %param.51) | copy-start | bytes 294916
  12.7 280.9 %copy-start.140 = (bf16[1536,32]{0,1:T(8,128)(2,1)S(1)}, bf16[1536,32]{0,1:T(8,128)(2,1)}, u32[]{:S(2)}) copy-start(bf16[1536,32]{0,1:T(8,128)(2,1)} %param.53) | copy-start | bytes 294916
  12.7 303.6 %copy-start.141 = (bf16[32,1536]{1,0:T(8,128)(2,1)S(1)}, bf16[32,1536]{1,0:T(8,128)(2,1)}, u32[]{:S(2)}) copy-start(bf16[32,1536]{1,0:T(8,128)(2,1)} %param.58) | copy-start | bytes 294916
  12.8 1311.7 %all-gather.38.cloned.1.call-start = ((), (), s32[]{:S(2)}) async-start(), calls=%async_computation.9 | async-start | bytes 17694720 | tf_op jit(solution)/shard_map/all_gather | solution.py:250
  13.5 323.0 %copy-start.142 = (bf16[32,1536]{1,0:T(8,128)(2,1)S(1)}, bf16[32,1536]{1,0:T(8,128)(2,1)}, u32[]{:S(2)}) copy-start(bf16[32,1536]{1,0:T(8,128)(2,1)} %param.64) | copy-start | bytes 294916
  13.5 339.3 %copy-start.143 = (bf16[1536,32]{0,1:T(8,128)(2,1)S(1)}, bf16[1536,32]{0,1:T(8,128)(2,1)}, u32[]{:S(2)}) copy-start(bf16[1536,32]{0,1:T(8,128)(2,1)} %param.61) | copy-start | bytes 294916
  13.5 358.4 %copy-start.144 = (bf16[1536,32]{0,1:T(8,128)(2,1)S(1)}, bf16[1536,32]{0,1:T(8,128)(2,1)}, u32[]{:S(2)}) copy-start(bf16[1536,32]{0,1:T(8,128)(2,1)} %param.59) | copy-start | bytes 294916
  13.5 374.5 %copy-start.130 = (bf16[32,2048]{1,0:T(8,128)(2,1)S(1)}, bf16[32,2048]{1,0:T(8,128)(2,1)}, u32[]{:S(2)}) copy-start(bf16[32,2048]{1,0:T(8,128)(2,1)} %param.52) | copy-start | bytes 393220
  13.5 1340.9 %all-gather.40.cloned.1.call-start = ((), (), s32[]{:S(2)}) async-start(), calls=%async_computation.10 | async-start | bytes 1474560 | tf_op jit(solution)/shard_map/all_gather | solution.py:185
  14.1 397.8 %copy-start.131 = (bf16[2048,32]{0,1:T(8,128)(2,1)S(1)}, bf16[2048,32]{0,1:T(8,128)(2,1)}, u32[]{:S(2)}) copy-start(bf16[2048,32]{0,1:T(8,128)(2,1)} %param.55) | copy-start | bytes 393220
  14.1 414.2 %copy-start.132 = (bf16[32,2048]{1,0:T(8,128)(2,1)S(1)}, bf16[32,2048]{1,0:T(8,128)(2,1)}, u32[]{:S(2)}) copy-start(bf16[32,2048]{1,0:T(8,128)(2,1)} %param.54) | copy-start | bytes 393220
  14.1 434.7 %copy-start.133 = (bf16[2048,32]{0,1:T(8,128)(2,1)S(1)}, bf16[2048,32]{0,1:T(8,128)(2,1)}, u32[]{:S(2)}) copy-start(bf16[2048,32]{0,1:T(8,128)(2,1)} %param.57) | copy-start | bytes 393220
  14.2 1585.0 %all-gather.34.cloned.1.call-start = ((), (), s32[]{:S(2)}) async-start(), calls=%async_computation.7 | async-start | bytes 17694720 | tf_op jit(solution)/shard_map/all_gather | solution.py:249
  14.9 1614.3 %all-gather.36.cloned.1.call-start = ((), (), s32[]{:S(2)}) async-start(), calls=%async_computation.8 | async-start | bytes 1474560 | tf_op jit(solution)/shard_map/all_gather | solution.py:184
  14.9 464.6 %collective-permute-start = (bf16[1536,1152]{1,0:T(8,128)(2,1)}, bf16[1536,1152]{1,0:T(8,128)(2,1)}, u32[]{:S(2)}, u32[]{:S(2)}) collective-permute-start(bf16[1536,1152]{1,0:T(8,128)(2,1)} %param.48), channel_id=1, source_target_pairs={{0,3},{1,0},{2,1},{3,2},{4,7},{5,4},{6,5},{7,6},{8,11},{9,8},{10,9... | collective-permute-start | bytes 10616840 | tf_op jit(solution)/shard_map/ppermute | solution.py:132
  20.1 2633.5 %all-reduce.96.cloned.1.call-start = ((), (), s32[]{:S(2)}) async-start(), calls=%async_computation.14 | async-start | bytes 36175872 | tf_op jit(solution)/shard_map/psum | solution.py:336
  22.9 456.6 %copy-start.166 = (f32[512]{0:T(512)}, f32[512]{0:T(512)S(1)}, u32[]{:S(2)}) copy-start(f32[512]{0:T(512)S(1)} %get-tuple-element.147) | copy-start | bytes 6148
  22.9 456.6 %copy-start.168 = (f32[512]{0:T(512)}, f32[512]{0:T(512)S(1)}, u32[]{:S(2)}) copy-start(f32[512]{0:T(512)S(1)} %get-tuple-element.148) | copy-start | bytes 6148
  22.9 456.6 %copy-start.170 = (f32[512]{0:T(512)}, f32[512]{0:T(512)S(1)}, u32[]{:S(2)}) copy-start(f32[512]{0:T(512)S(1)} %get-tuple-element.149) | copy-start | bytes 6148
  201.9 302.0 %copy-start.148 = (f32[1536]{0:T(1024)}, f32[1536]{0:T(1024)S(1)}, u32[]{:S(2)}) copy-start(f32[1536]{0:T(1024)S(1)} %reshape.246) | copy-start | bytes 18436
  273.1 222.5 %copy-start.177 = (s32[1024]{0:T(1024)}, s32[1024]{0:T(1024)S(1)}, u32[]{:S(2)}) copy-start(s32[1024]{0:T(1024)S(1)} %pad_clamp_fusion.1) | copy-start | bytes 12292
  474.1 29.9 copy-start.159
  474.7 97.2 %copy-start.128 = (f32[2048]{0:T(1024)}, f32[2048]{0:T(1024)S(1)}, u32[]{:S(2)}) copy-start(f32[2048]{0:T(1024)S(1)} %get-tuple-element.145) | copy-start | bytes 24580
  475.4 37.4 %copy-start.146 = (f32[1,2048]{1,0:T(1,128)}, f32[1,2048]{1,0:T(1,128)S(1)}, u32[]{:S(2)}) copy-start(f32[1,2048]{1,0:T(1,128)S(1)} %get-tuple-element.140) | copy-start | bytes 24580
  486.0 600.0 %collective-permute-start.1 = (bf16[1536,2304]{1,0:T(8,128)(2,1)}, bf16[1536,2304]{1,0:T(8,128)(2,1)}, u32[]{:S(2)}, u32[]{:S(2)}) collective-permute-start(bf16[1536,2304]{1,0:T(8,128)(2,1)} %pad_maximum_fusion), channel_id=1, source_target_pairs={{0,2},{1,3},{2,0},{3,1},{4,6},{5,7},{6,4},{7,5},{8,10},{9,11},{10,... | collective-permute-start | bytes 21233672 | tf_op jit(solution)/shard_map/ppermute | solution.py:132
  503.3 544.7 %copy-start.14 = (bf16[512,1536]{1,0:T(8,128)(2,1)}, bf16[512,1536]{1,0:T(8,128)(2,1)S(1)}, u32[]{:S(2)}) copy-start(bf16[512,1536]{1,0:T(8,128)(2,1)S(1)} %gather_fusion) | copy-start | bytes 4718596
  505.6 392.3 %copy-start.9 = (bf16[512,1536]{1,0:T(8,128)(2,1)}, bf16[512,1536]{1,0:T(8,128)(2,1)S(1)}, u32[]{:S(2)}) copy-start(bf16[512,1536]{1,0:T(8,128)(2,1)S(1)} %fusion.46) | copy-start | bytes 4718596
  690.3 58.1 %copy-start.83 = (f32[16,2048]{1,0:T(8,128)}, f32[16,2048]{1,0:T(8,128)S(1)}, u32[]{:S(2)}) copy-start(f32[16,2048]{1,0:T(8,128)S(1)} %slice.348) | copy-start | bytes 393220
  718.5 45.7 %copy-start.126 = (f32[2,2048]{1,0:T(2,128)}, f32[2,2048]{1,0:T(2,128)S(1)}, u32[]{:S(2)}) copy-start(f32[2,2048]{1,0:T(2,128)S(1)} %slice.366) | copy-start | bytes 49156
  757.0 25.0 copy-start.78
  866.7 16.6 copy-start.178
  903.6 144.4 %copy-start.160 = (pred[512]{0:T(512)(128)(4,1)S(1)}, pred[512]{0:T(512)(128)(4,1)}, u32[]{:S(2)}) copy-start(pred[512]{0:T(512)(128)(4,1)} %copy-done.159) | copy-start | bytes 1540
  910.3 144.4 %copy-start.100 = (bf16[512,128]{1,0:T(8,128)(2,1)}, bf16[512,128]{1,0:T(8,128)(2,1)S(1)}, u32[]{:S(2)}) copy-start(bf16[512,128]{1,0:T(8,128)(2,1)S(1)} %fusion.56) | copy-start | bytes 393220
  1055.4 652.6 %copy-start.4 = (f32[512,1536]{1,0:T(8,128)}, f32[512,1536]{1,0:T(8,128)S(1)}, u32[]{:S(2)}) copy-start(f32[512,1536]{1,0:T(8,128)S(1)} %get-tuple-element.154) | copy-start | bytes 9437188
  1057.5 571.7 %copy-start.87 = (bf16[512,128]{1,0:T(8,128)(2,1)}, bf16[512,128]{1,0:T(8,128)(2,1)S(1)}, u32[]{:S(2)}) copy-start(bf16[512,128]{1,0:T(8,128)(2,1)S(1)} %fusion.62) | copy-start | bytes 393220
  1638.4 34.7 %copy-start.52 = (bf16[128,4608]{1,0:T(8,128)(2,1)S(1)}, bf16[128,4608]{1,0:T(8,128)(2,1)}, u32[]{:S(2)}) copy-start(bf16[128,4608]{1,0:T(8,128)(2,1)} %all-gather.32.cloned.1.call-done) | copy-start | bytes 3538948
  1723.4 20.1 copy-start.17
  1788.0 14.6 copy-start.37
  1806.3 19.5 copy-start.81
  1809.1 19.4 copy-start.29
  1809.1 19.4 copy-start.31
  1809.1 19.4 slice-start.10
  1844.6 22.3 copy-start.55
  1849.6 22.1 copy-start.19
  1849.6 22.1 slice-start.9
  1901.7 16.7 copy-start.33
  1944.0 16.7 copy-start.32
  2041.9 24.7 slice-start.6
  2081.0 795.7 %all-gather.46.cloned.1.call-start = ((), (), s32[]{:S(2)}) async-start(), calls=%async_computation.13 | async-start | bytes 15728640 | tf_op jit(solution)/shard_map/all_gather | solution.py:325
  2099.0 996.2 %all-gather.42.cloned.1.call-start = ((), (), s32[]{:S(2)}) async-start(), calls=%async_computation.11 | async-start | bytes 15728640 | tf_op jit(solution)/shard_map/all_gather | solution.py:324
  (160 other events, 747.5 us)
Sparse Core Ops, SparseCore 0:
  9.6 187.8 all-gather.19
  199.1 139.9 all-gather.21
  340.6 35.2 all-gather.23
  377.3 37.8 all-gather.25
  416.6 315.6 all-gather.43
  733.7 164.1 all-gather.27
  899.5 148.5 all-gather.29
  1049.6 30.0 all-gather.31
  1081.3 243.0 all-gather.37
  1325.8 28.6 all-gather.39
  1356.1 243.0 all-gather.33
  1600.6 28.6 all-gather.35
  2081.1 572.3 all-reduce.95
  2657.1 219.4 all-gather.45
  2878.7 216.3 all-gather.41
